TPU v7x, 256 devices: a whole 4x4x8 slice. The times are simulated.
256 devices in a mesh: tok: 16 (over y, x), ch: 16 (over z, core).
Axes of the slice: x: 4, y: 4, z: 8, core: 2. Of those that a mesh axis runs over, the one named last changes fastest.
Arguments:
- tokens: bfloat16 [256, 16384], P('tok', 'ch'), may hold values from -64 to 64
- probe: int32 [256, 16384], P('tok', 'ch'), may hold values from 0 to 1
- signs: int32 [16384], P('ch'), may hold values from 0 to 1
- gate_weight: bfloat16 [16384, 26624], P('ch', 'tok'), may hold values from -0.046875 to 0.046875
- up_weight: bfloat16 [16384, 26624], P('ch', 'tok'), may hold values from -0.046875 to 0.046875
- down_weight: bfloat16 [26624, 16384], P('tok', 'ch'), may hold values from -0.0390625 to 0.0390625
Outputs:
- rotated_product: float32 [256, 16384], P('tok', 'ch')
- diagonal_estimate: float32 [16384], P('ch')
All inputs are finite; a program needn't handle non-finite values.
Results may differ from a plain program's by a relative error of at most 0.004.
Values may be sent and summed in bfloat16 or wider, within the bound.
No kernel may reach another device: no remote copies, remote signals or barrier semaphores. Data moves between devices by JAX's collectives and lax.ppermute only.
A program may use at most 128 MiB of HBM per device.

v0:
```python
import math
import jax
import jax.numpy as jnp
import numpy as np
from jax import lax
from jax.sharding import PartitionSpec as P

D = 16384
LANES = 128
F32 = jnp.float32
BF16 = jnp.bfloat16


def sign_table(length):
    table = np.ones((1, 1), np.float32)
    while table.shape[0] < length:
        table = np.block([[table, table], [table, -table]])
    return table


def swap(value, mask):
    pairs = [(source, source ^ mask) for source in range(lax.axis_size("ch"))]
    return lax.ppermute(value, "ch", pairs)


def cross(values, my_index):
    for bit_pos in range(lax.axis_size("ch").bit_length() - 1):
        partner = swap(values, 2**bit_pos)
        upper = my_index >> bit_pos & 1 == 1
        values = jnp.where(upper, partner - values, values + partner)
    return values


def local_transform(values, table, precision=None):
    rows, length = values.shape
    groups = [values[:, at : at + LANES] for at in range(0, length, LANES)]
    step = 1
    while step < len(groups):
        for low in range(len(groups)):
            if not low & step:
                first, second = (groups[low], groups[low + step])
                groups[low], groups[low + step] = (first + second, first - second)
        step *= 2
    stacked = jnp.concatenate(groups, axis=0)
    done = jnp.dot(
        stacked, table.astype(values.dtype), precision=precision, preferred_element_type=F32
    )
    return jnp.concatenate([done[at : at + rows] for at in range(0, done.shape[0], rows)], axis=1)


def gather_tok(value):
    size = lax.axis_size("tok")
    copies = jnp.broadcast_to(value[None], (size,) + value.shape)
    return lax.all_to_all(copies, "tok", 0, 0, tiled=True)


def scatter_tok(value, send_type):
    size = lax.axis_size("tok")
    blocks = value.astype(send_type).reshape(size, value.shape[0] // size, value.shape[1])
    arrived = lax.all_to_all(blocks, "tok", 0, 0, tiled=True)
    return jnp.sum(arrived.astype(F32), axis=0)


def chip_groups():
    size = lax.axis_size("ch")
    return [[chip + core for chip in range(0, size, 2)] for core in range(2)]


def rows_of_core(value, core):
    size = lax.axis_size("ch")
    blocks = value.reshape(size // 2, 2, value.shape[0] // size, value.shape[1])
    chosen = lax.dynamic_index_in_dim(blocks, core, 1, keepdims=False)
    return chosen.reshape(value.shape[0] // 2, value.shape[1])


def scatter_ch(product, rows, core, swap_type, send_type):
    theirs = product(rows_of_core(rows, 1 - core)).astype(swap_type)
    arrived = swap(theirs, 1)
    mine = product(rows_of_core(rows, core))
    both = (mine + arrived.astype(F32)).astype(send_type)
    chips = lax.axis_size("ch") // 2
    blocks = both.reshape(chips, both.shape[0] // chips, both.shape[1])
    pieces = lax.all_to_all(blocks, "ch", 0, 0, tiled=True, axis_index_groups=chip_groups())
    return jnp.sum(pieces.astype(F32), axis=0)


def times(rows, weight):
    return jnp.dot(rows, weight, preferred_element_type=F32)


def times_t(rows, weight):
    return lax.dot_general(rows, weight, (((1,), (1,)), ((), ())), preferred_element_type=F32)


def on_device(tokens, probe, signs, gate_weight, up_weight, down_weight):
    tok_rows, channels = tokens.shape
    total_rows = tok_rows * lax.axis_size("tok")
    hidden = gate_weight.shape[1]
    my_index = lax.axis_index("ch")
    core = my_index & 1
    root_scale = 1.0 / math.sqrt(D)
    table = jnp.asarray(sign_table(LANES))
    probe_signs = (2 * probe - 1).astype(F32)
    channel_signs = (2 * signs - 1).astype(F32)
    all_tokens = gather_tok(tokens).reshape(total_rows, channels)
    token_part = jnp.stack([times(all_tokens, gate_weight), times(all_tokens, up_weight)], axis=1)
    token_sum = lax.psum_scatter(token_part, "ch", scatter_dimension=0, tiled=True)
    crossed = cross((probe_signs * channel_signs[None, :]).astype(BF16), my_index)
    tangent = (
        local_transform(crossed.astype(F32), table, lax.Precision.HIGHEST) * root_scale
    ).astype(BF16)
    all_tangent = gather_tok(tangent).reshape(total_rows, channels)

    def gate_and_up(rows):
        return jnp.concatenate([times(rows, gate_weight), times(rows, up_weight)], axis=1)

    tangent_sum = scatter_ch(gate_and_up, all_tangent, core, BF16, BF16)
    gate_pre, up_pre = (token_sum[:, 0], token_sum[:, 1])
    gate_tan, up_tan = (tangent_sum[:, :hidden], tangent_sum[:, hidden:])
    sigmoid_gate = jax.nn.sigmoid(gate_pre)
    activated = gate_pre * sigmoid_gate
    slope_term = sigmoid_gate * (1.0 + gate_pre * (1.0 - sigmoid_gate))
    hidden_tan = (slope_term * gate_tan * up_pre + activated * up_tan).astype(BF16)
    out_part = times(lax.all_gather(hidden_tan, "ch", axis=0, tiled=True), down_weight)
    out_tangent = scatter_tok(out_part, F32).astype(BF16)
    all_out = gather_tok(out_tangent).reshape(total_rows, channels)
    back_hidden = scatter_ch(lambda rows: times_t(rows, down_weight), all_out, core, F32, BF16)
    back_gate = (back_hidden * up_pre * slope_term).astype(BF16)
    back_up = (back_hidden * activated).astype(BF16)
    back = jnp.concatenate([back_gate, back_up], axis=1)
    mine = lax.all_gather(back, "ch", axis=0, tiled=True, axis_index_groups=chip_groups())
    theirs = swap(mine, 1)

    def grad(rows):
        return times_t(rows[:, :hidden], gate_weight) + times_t(rows[:, hidden:], up_weight)

    in_mine, in_theirs = (grad(mine), grad(theirs))
    split = (lax.axis_size("ch") // 2, tok_rows, channels)
    in_mine, in_theirs = (in_mine.reshape(split), in_theirs.reshape(split))
    first = core == 0
    in_part = jnp.stack(
        [jnp.where(first, in_mine, in_theirs), jnp.where(first, in_theirs, in_mine)], axis=1
    ).reshape(total_rows, channels)
    back_tokens = scatter_tok(in_part, F32)
    local_back = local_transform(back_tokens, table, lax.Precision.HIGHEST)
    rotated_product = cross(local_back, my_index) * root_scale * channel_signs[None, :]
    token_terms = jnp.sum(probe_signs * rotated_product, axis=0)
    pieces = gather_tok(token_terms.reshape(-1, LANES))
    pieces = pieces.reshape(lax.axis_size("tok"), channels // LANES, LANES)
    diagonal_estimate = jnp.sum(pieces, axis=0).reshape(channels) / total_rows
    return (rotated_product, diagonal_estimate)


def solution(mesh):
    placed = (
        P("tok", "ch"),
        P("tok", "ch"),
        P("ch"),
        P("ch", "tok"),
        P("ch", "tok"),
        P("tok", "ch"),
    )
    return jax.shard_map(
        on_device, mesh=mesh, in_specs=placed, out_specs=(P("tok", "ch"), P("ch")), check_vma=False
    )
```

profile of v0, /device:TPU:2, one launch (start us, length us, event | category | flops | bytes accessed | tf_op | source)
XLA Modules:
  0.0 309.4 jit_solution(1250894216051346519)
XLA Ops:
  7.2 0.8 add_convert_fusion
  8.0 1.0 multiply_convert_fusion.3
  9.1 0.1 collective-permute-start
  9.2 1.2 collective-permute-done
  10.4 0.9 add_select_fusion.5
  11.2 2.0 collective-permute-start.1
  13.2 2.0 collective-permute-done.1
  15.2 3.4 %collective-permute-start.2 = (bf16[16,1024]{1,0:T(8,128)(2,1)S(1)}, bf16[16,1024]{1,0:T(8,128)(2,1)S(1)}, u32[]{:S(2)}, u32[]{:S(2)}) collective-permute-start(bf16[16,1024]{1,0:T(8,128)(2,1)S(1)} %add_select_fusion.4), channel_id=1, source_target_pairs={{0,4},{1,5},{2,6},{3,7},{4,0},{5,1},{6,2},{7,3},{8,12},{9,13},{10,... | collective-permute-start | bytes 98312 | tf_op jit(solution)/shard_map/ppermute | solution.py:23
  18.6 1.9 collective-permute-done.2
  20.5 6.9 %collective-permute-start.3 = (bf16[16,1024]{1,0:T(8,128)(2,1)S(1)}, bf16[16,1024]{1,0:T(8,128)(2,1)S(1)}, u32[]{:S(2)}, u32[]{:S(2)}) collective-permute-start(bf16[16,1024]{1,0:T(8,128)(2,1)S(1)} %add_select_fusion.3), channel_id=1, source_target_pairs={{0,8},{1,9},{2,10},{3,11},{4,12},{5,13},{6,14},{7,15},{8,0},{9,1},... | collective-permute-start | bytes 98312 | tf_op jit(solution)/shard_map/ppermute | solution.py:23
  27.4 1.6 broadcast_in_dim.10
  29.1 7.5 %all-to-all-start = ((bf16[16,16,1024]{2,1,0:T(8,128)(2,1)}), bf16[16,16,1024]{2,1,0:T(8,128)(2,1)}, u32[]{:S(2)}, u32[]{:S(2)}) async-start(bf16[16,16,1024]{2,1,0:T(8,128)(2,1)} %broadcast_in_dim.10), calls=%async_computation | async-start | bytes 1048576 | tf_op jit(solution)/shard_map/all_to_all | solution.py:54
  36.7 1.0 fusion.12
  37.8 7.6 %all-to-all-done = bf16[16,16,1024]{2,1,0:T(8,128)(2,1)} async-done(((bf16[16,16,1024]{2,1,0:T(8,128)(2,1)}), bf16[16,16,1024]{2,1,0:T(8,128)(2,1)}, u32[]{:S(2)}, u32[]{:S(2)}) %all-to-all-start) | async-done | bytes 524320 | tf_op jit(solution)/shard_map/all_to_all | solution.py:54
  45.4 3.2 %convolution_bitcast_fusion = f32[256,1,1664]{2,0,1:T(8,128)S(1)} fusion(bf16[256,1024]{1,0:T(8,128)(2,1)} %bitcast, bf16[1024,1664]{1,0:T(8,128)(2,1)} %param.11), kind=kOutput, calls=%fused_computation.1 | convolution fusion | flops 872415232 | bytes 5636096 | tf_op jit(solution)/shard_map/dot_general | solution.py:88
  48.7 2.2 convolution_bitcast_fusion.1
  50.8 1.9 pad_maximum_fusion
  52.9 0.8 broadcast_in_dim.11
  53.7 5.4 %all-to-all-start.1 = ((bf16[16,16,1024]{2,1,0:T(8,128)(2,1)}), bf16[16,16,1024]{2,1,0:T(8,128)(2,1)}, u32[]{:S(2)}, u32[]{:S(2)}) async-start(bf16[16,16,1024]{2,1,0:T(8,128)(2,1)} %broadcast_in_dim.11), calls=%async_computation.2 | async-start | bytes 1048576 | tf_op jit(solution)/shard_map/all_to_all | solution.py:54
  59.2 9.0 %all-to-all-done.1 = bf16[16,16,1024]{2,1,0:T(8,128)(2,1)} async-done(((bf16[16,16,1024]{2,1,0:T(8,128)(2,1)}), bf16[16,16,1024]{2,1,0:T(8,128)(2,1)}, u32[]{:S(2)}, u32[]{:S(2)}) %all-to-all-start.1) | async-done | bytes 524320 | tf_op jit(solution)/shard_map/all_to_all | solution.py:54
  68.1 1.1 constant_dynamic-slice_fusion.2
  69.2 2.6 convolution_convert_fusion
  71.9 0.7 convolution_convert_fusion.1
  72.5 0.1 pad_maximum_fusion.2
  72.6 0.1 collective-permute-start.4
  72.7 0.7 fusion.13
  73.4 1.2 copy-done.1
  74.5 0.7 fusion.14
  75.2 0.1 fusion.1
  75.3 32.4 %all_to_all.40 = bf16[8,16,3328]{2,1,0:T(8,128)(2,1)S(1)} all-to-all(bf16[8,16,3328]{2,1,0:T(8,128)(2,1)S(1)} %bitcast.71), channel_id=1, replica_groups={{0,2,4,6,8,10,12,14},{1,3,5,7,9,11,13,15},{16,18,20,22,24,26,28,30},{17..., dimensions={0} | all-to-all | bytes 1703936 | tf_op jit(solution)/shard_map/all_to_all | solution.py:83
  107.7 0.8 convert_reduce_fusion
  108.6 12.0 %reduce-scatter.2.cloned.1.call-done = f32[16,2,1664]{2,0,1:T(8,128)} async-done(((f32[256,2,1664]{2,0,1:T(8,128)}), f32[16,2,1664]{2,0,1:T(8,128)}) %reduce-scatter.2.cloned.1.call-update) | async-done | bytes 213008 | tf_op jit(solution)/shard_map/reduce_scatter | solution.py:107
  120.6 1.1 fusion.9
  121.7 17.1 %all_gather.6 = bf16[256,1664]{1,0:T(8,128)(2,1)S(1)} all-gather(bf16[16,1664]{1,0:T(8,128)(2,1)S(1)} %fusion.9), channel_id=1, replica_groups=mesh['tok'=16,'ch'=16] {'ch'}, dimensions={0}, use_global_device_ids=true | all-gather | bytes 905216 | tf_op jit(solution)/shard_map/all_gather | solution.py:124
  138.8 3.1 %fusion.15 = f32[256,1024]{1,0:T(8,128)S(1)} fusion(bf16[256,1664]{1,0:T(8,128)(2,1)S(1)} %all_gather.6, bf16[1664,1024]{1,0:T(8,128)(2,1)} %param.12), kind=kOutput, calls=%fused_computation.106 | convolution fusion | flops 872415232 | bytes 5308416 | tf_op jit(solution)/shard_map/dot_general | solution.py:88
  141.9 23.0 %all_to_all.41 = f32[16,16,1024]{2,1,0:T(8,128)} all-to-all(f32[16,16,1024]{2,1,0:T(8,128)S(1)} %bitcast.82), channel_id=1, replica_groups=mesh['tok'=16,'ch'=16] {'tok'}, dimensions={0} | all-to-all | bytes 2097152 | tf_op jit(solution)/shard_map/all_to_all | solution.py:60
  164.9 1.3 reduce_sum.55
  166.3 14.2 %all_to_all.42 = bf16[16,16,1024]{2,1,0:T(8,128)(2,1)S(1)} all-to-all(bf16[16,16,1024]{2,1,0:T(8,128)(2,1)S(1)} %broadcast_in_dim.12), channel_id=1, replica_groups=mesh['tok'=16,'ch'=16] {'tok'}, dimensions={0} | all-to-all | bytes 1048576 | tf_op jit(solution)/shard_map/all_to_all | solution.py:54
  180.5 3.2 %fusion.16 = f32[128,1664]{1,0:T(8,128)S(1)} fusion(bf16[128,1024]{1,0:T(8,128)(2,1)S(1)} %bitcast.81, bf16[1664,1024]{1,0:T(8,128)(2,1)} %param.12), kind=kOutput, calls=%fused_computation.107 | convolution fusion | flops 436207616 | bytes 4521984 | tf_op jit(solution)/shard_map/dot_general | solution.py:92
  183.7 0.3 collective-permute-start.5
  184.0 2.4 collective-permute-done.5
  186.3 1.2 fusion
  187.6 21.8 %all_to_all.43 = bf16[8,16,1664]{2,1,0:T(8,128)(2,1)S(1)} all-to-all(bf16[8,16,1664]{2,1,0:T(8,128)(2,1)S(1)} %bitcast.79), channel_id=1, replica_groups={{0,2,4,6,8,10,12,14},{1,3,5,7,9,11,13,15},{16,18,20,22,24,26,28,30},{17..., dimensions={0} | all-to-all | bytes 851968 | tf_op jit(solution)/shard_map/all_to_all | solution.py:83
  209.4 0.1 multiply_convert_fusion.1
  209.5 28.2 %all_gather.7 = bf16[128,3328]{1,0:T(8,128)(2,1)} all-gather(bf16[16,3328]{1,0:T(8,128)(2,1)S(1)} %pad_maximum_fusion.3), channel_id=1, replica_groups={{0,2,4,6,8,10,12,14},{1,3,5,7,9,11,13,15},{16,18,20,22,24,26,28,30},{17..., dimensions={0}, use_global_device_ids=true | all-gather | bytes 958464 | tf_op jit(solution)/shard_map/all_gather | solution.py:131
  237.8 2.4 fusion.6
  240.1 2.2 convolution_add_fusion.2
  242.4 2.2 fusion.2
  244.6 2.2 broadcast_select_fusion.1
  246.9 0.1 pad_maximum_fusion.1
  247.0 21.5 %all_to_all.44 = f32[16,16,1024]{2,1,0:T(8,128)} all-to-all(f32[16,16,1024]{2,1,0:T(8,128)S(1)} %bitcast.70), channel_id=1, replica_groups=mesh['tok'=16,'ch'=16] {'tok'}, dimensions={0} | all-to-all | bytes 2097152 | tf_op jit(solution)/shard_map/all_to_all | solution.py:60
  268.4 1.3 reduce_sum.57
  269.9 1.0 fusion.17
  271.0 0.1 collective-permute-start.7
  271.1 1.2 collective-permute-done.7
  272.3 0.1 collective-permute-start.8
  272.4 4.3 %collective-permute-done.8 = f32[16,1024]{1,0:T(8,128)S(1)} collective-permute-done((f32[16,1024]{1,0:T(8,128)S(1)}, f32[16,1024]{1,0:T(8,128)S(1)}, u32[]{:S(2)}, u32[]{:S(2)}) %collective-permute-start.8) | collective-permute-done | bytes 65568 | tf_op jit(solution)/shard_map/ppermute | solution.py:23
  276.7 0.3 collective-permute-start.9
  277.0 5.2 %collective-permute-done.9 = f32[16,1024]{1,0:T(8,128)S(1)} collective-permute-done((f32[16,1024]{1,0:T(8,128)S(1)}, f32[16,1024]{1,0:T(8,128)S(1)}, u32[]{:S(2)}, u32[]{:S(2)}) %collective-permute-start.9) | collective-permute-done | bytes 65568 | tf_op jit(solution)/shard_map/ppermute | solution.py:23
  282.3 1.7 collective-permute-start.10
  284.0 6.6 %collective-permute-done.10 = f32[16,1024]{1,0:T(8,128)S(1)} collective-permute-done((f32[16,1024]{1,0:T(8,128)S(1)}, f32[16,1024]{1,0:T(8,128)S(1)}, u32[]{:S(2)}, u32[]{:S(2)}) %collective-permute-start.10) | collective-permute-done | bytes 65568 | tf_op jit(solution)/shard_map/ppermute | solution.py:23
  290.6 0.7 multiply_reduce_fusion
  291.2 10.7 %all_to_all.45 = f32[16,8,128]{2,1,0:T(8,128)S(1)} all-to-all(f32[16,8,128]{2,1,0:T(8,128)S(1)} %broadcast_in_dim.14), channel_id=1, replica_groups=mesh['tok'=16,'ch'=16] {'tok'}, dimensions={0} | all-to-all | bytes 131072 | tf_op jit(solution)/shard_map/all_to_all | solution.py:54
  302.0 0.6 multiply_bitcast_fusion
  (65 shorter events, 0.5 us)
Async XLA Ops:
  7.2 41.5 %copy-start = (bf16[1024,1664]{1,0:T(8,128)(2,1)S(1)}, bf16[1024,1664]{1,0:T(8,128)(2,1)}, u32[]{:S(2)}) copy-start(bf16[1024,1664]{1,0:T(8,128)(2,1)} %param.10) | copy-start | bytes 10223620
  9.1 1.3 collective-permute-start
  11.2 4.0 %collective-permute-start.1 = (bf16[16,1024]{1,0:T(8,128)(2,1)S(1)}, bf16[16,1024]{1,0:T(8,128)(2,1)S(1)}, u32[]{:S(2)}, u32[]{:S(2)}) collective-permute-start(bf16[16,1024]{1,0:T(8,128)(2,1)S(1)} %add_select_fusion.5), channel_id=1, source_target_pairs={{0,2},{1,3},{2,0},{3,1},{4,6},{5,7},{6,4},{7,5},{8,10},{9,11},{10,... | collective-permute-start | bytes 98312 | tf_op jit(solution)/shard_map/ppermute | solution.py:23
  15.2 5.3 %collective-permute-start.2 = (bf16[16,1024]{1,0:T(8,128)(2,1)S(1)}, bf16[16,1024]{1,0:T(8,128)(2,1)S(1)}, u32[]{:S(2)}, u32[]{:S(2)}) collective-permute-start(bf16[16,1024]{1,0:T(8,128)(2,1)S(1)} %add_select_fusion.4), channel_id=1, source_target_pairs={{0,4},{1,5},{2,6},{3,7},{4,0},{5,1},{6,2},{7,3},{8,12},{9,13},{10,... | collective-permute-start | bytes 98312 | tf_op jit(solution)/shard_map/ppermute | solution.py:23
  20.5 16.1 %collective-permute-start.3 = (bf16[16,1024]{1,0:T(8,128)(2,1)S(1)}, bf16[16,1024]{1,0:T(8,128)(2,1)S(1)}, u32[]{:S(2)}, u32[]{:S(2)}) collective-permute-start(bf16[16,1024]{1,0:T(8,128)(2,1)S(1)} %add_select_fusion.3), channel_id=1, source_target_pairs={{0,8},{1,9},{2,10},{3,11},{4,12},{5,13},{6,14},{7,15},{8,0},{9,1},... | collective-permute-start | bytes 98312 | tf_op jit(solution)/shard_map/ppermute | solution.py:23
  29.1 16.4 %all-to-all-start = ((bf16[16,16,1024]{2,1,0:T(8,128)(2,1)}), bf16[16,16,1024]{2,1,0:T(8,128)(2,1)}, u32[]{:S(2)}, u32[]{:S(2)}) async-start(bf16[16,16,1024]{2,1,0:T(8,128)(2,1)} %broadcast_in_dim.10), calls=%async_computation | async-start | bytes 1048576 | tf_op jit(solution)/shard_map/all_to_all | solution.py:54
  36.5 84.1 %reduce-scatter.2.cloned.1.call-start = ((), (), s32[]{:S(2)}) async-start(), calls=%async_computation.9 | async-start | bytes 3620864 | tf_op jit(solution)/shard_map/reduce_scatter | solution.py:107
  53.7 14.4 %all-to-all-start.1 = ((bf16[16,16,1024]{2,1,0:T(8,128)(2,1)}), bf16[16,16,1024]{2,1,0:T(8,128)(2,1)}, u32[]{:S(2)}, u32[]{:S(2)}) async-start(bf16[16,16,1024]{2,1,0:T(8,128)(2,1)} %broadcast_in_dim.11), calls=%async_computation.2 | async-start | bytes 1048576 | tf_op jit(solution)/shard_map/all_to_all | solution.py:54
  72.5 2.0 copy-start.1
  72.6 2.6 collective-permute-start.4
  166.3 20.1 %copy-start.3 = (bf16[1664,1024]{1,0:T(8,128)(2,1)S(1)}, bf16[1664,1024]{1,0:T(8,128)(2,1)}, u32[]{:S(2)}) copy-start(bf16[1664,1024]{1,0:T(8,128)(2,1)} %param.12) | copy-start | bytes 10223620
  183.7 25.8 %copy-start.4 = (f32[16,2,1664]{2,0,1:T(8,128)S(1)}, f32[16,2,1664]{2,0,1:T(8,128)}, u32[]{:S(2)}) copy-start(f32[16,2,1664]{2,0,1:T(8,128)} %reduce-scatter.2.cloned.1.call-done) | copy-start | bytes 638980
  183.7 2.6 collective-permute-start.5
  237.7 4.6 %collective-permute-start.6 = (bf16[128,3328]{1,0:T(8,128)(2,1)}, bf16[128,3328]{1,0:T(8,128)(2,1)}, u32[]{:S(2)}, u32[]{:S(2)}) collective-permute-start(bf16[128,3328]{1,0:T(8,128)(2,1)} %all_gather.7), channel_id=1, source_target_pairs={{0,1},{1,0},{2,3},{3,2},{4,5},{5,4},{6,7},{7,6},{8,9},{9,8},{10,11... | collective-permute-start | bytes 2555912 | tf_op jit(solution)/shard_map/ppermute | solution.py:23
  237.8 2.4 copy-start.2
  246.9 37.1 %copy-start.6 = (s32[1024]{0:T(1024)S(1)}, s32[1024]{0:T(1024)}, u32[]{:S(2)}) copy-start(s32[1024]{0:T(1024)} %param.9) | copy-start | bytes 12292
  246.9 43.7 %copy-start.5 = (s32[16,1024]{1,0:T(8,128)S(1)}, s32[16,1024]{1,0:T(8,128)}, u32[]{:S(2)}) copy-start(s32[16,1024]{1,0:T(8,128)} %param.8) | copy-start | bytes 196612
  271.0 1.3 collective-permute-start.7
  272.3 4.4 %collective-permute-start.8 = (f32[16,1024]{1,0:T(8,128)S(1)}, f32[16,1024]{1,0:T(8,128)S(1)}, u32[]{:S(2)}, u32[]{:S(2)}) collective-permute-start(f32[16,1024]{1,0:T(8,128)S(1)} %add_select_fusion.2), channel_id=1, source_target_pairs={{0,2},{1,3},{2,0},{3,1},{4,6},{5,7},{6,4},{7,5},{8,10},{9,11},{10,... | collective-permute-start | bytes 196616 | tf_op jit(solution)/shard_map/ppermute | solution.py:23
  276.7 5.6 %collective-permute-start.9 = (f32[16,1024]{1,0:T(8,128)S(1)}, f32[16,1024]{1,0:T(8,128)S(1)}, u32[]{:S(2)}, u32[]{:S(2)}) collective-permute-start(f32[16,1024]{1,0:T(8,128)S(1)} %add_select_fusion.1), channel_id=1, source_target_pairs={{0,4},{1,5},{2,6},{3,7},{4,0},{5,1},{6,2},{7,3},{8,12},{9,13},{10,... | collective-permute-start | bytes 196616 | tf_op jit(solution)/shard_map/ppermute | solution.py:23
  282.3 8.3 %collective-permute-start.10 = (f32[16,1024]{1,0:T(8,128)S(1)}, f32[16,1024]{1,0:T(8,128)S(1)}, u32[]{:S(2)}, u32[]{:S(2)}) collective-permute-start(f32[16,1024]{1,0:T(8,128)S(1)} %add_select_fusion), channel_id=1, source_target_pairs={{0,8},{1,9},{2,10},{3,11},{4,12},{5,13},{6,14},{7,15},{8,0},{9,1},... | collective-permute-start | bytes 196616 | tf_op jit(solution)/shard_map/ppermute | solution.py:23
Sparse Core Ops, SparseCore 0:
  52.9 67.6 reduce-scatter.1
where the time goes:
time: 311 us; the launch traced here: 309 us
  blocking collectives  169 us (54%)
  waiting for transfers between devices  53.5 us (17%)
  matrix products  28.7 us (9%)
  starting transfers between devices  27.9 us (9%)
  between operations  14.6 us (5%)
  other arithmetic  11.1 us (4%)
  local copies, waits for them, and re-layouts  4.86 us (2%)
    all_to_all x2, blocking collectives, scatter_ch(): lax.all_to_all(blocks, 'ch', 0, 0, tiled=True, axis_index_groups=chip_gro...  54.2 us
    all_to_all x2, blocking collectives, scatter_tok(): arrived = lax.all_to_all(blocks, 'tok', 0, 0, tiled=True)  44.5 us
    all_gather x1, blocking collectives, on_device(): lax.all_gather(back, 'ch', axis=0, tiled=True, axis_index_groups=chip_gro...  28.2 us
    all_to_all x2, blocking collectives, gather_tok(): return lax.all_to_all(copies, 'tok', 0, 0, tiled=True)  24.9 us
    ppermute x11, waiting for transfers between devices, swap(): return lax.ppermute(value, 'ch', pairs)  24.8 us
    all_gather x1, blocking collectives, on_device(): lax.all_gather(hidden_tan, 'ch', axis=0, tiled=True)  17.1 us
    all_to_all x2, waiting for transfers between devices, gather_tok(): return lax.all_to_all(copies, 'tok', 0, 0, tiled=True)  16.6 us
    ppermute x11, starting transfers between devices, swap(): return lax.ppermute(value, 'ch', pairs)  14.9 us
  transfers between devices with their start and end apart: 14, of which 11 were waited for; matrix products, arithmetic and copies ran while one was open for 5% of the time, Pallas kernels for 0%

commit v1 on v0

--- a/solution.py
+++ b/solution.py
@@ -93,6 +93,12 @@
 
 
 def on_device(tokens, probe, signs, gate_weight, up_weight, down_weight):
+
+    def part_skins_by_axis(u_in):
+        return jnp.concatenate(
+            lax.all_to_all(jnp.stack([u_in] * lax.axis_size("ch"), 0), "ch", 0, 0), 0
+        )
+
     tok_rows, channels = tokens.shape
     total_rows = tok_rows * lax.axis_size("tok")
     hidden = gate_weight.shape[1]
@@ -121,7 +127,7 @@
     activated = gate_pre * sigmoid_gate
     slope_term = sigmoid_gate * (1.0 + gate_pre * (1.0 - sigmoid_gate))
     hidden_tan = (slope_term * gate_tan * up_pre + activated * up_tan).astype(BF16)
-    out_part = times(lax.all_gather(hidden_tan, "ch", axis=0, tiled=True), down_weight)
+    out_part = times(part_skins_by_axis(hidden_tan), down_weight)
     out_tangent = scatter_tok(out_part, F32).astype(BF16)
     all_out = gather_tok(out_tangent).reshape(total_rows, channels)
     back_hidden = scatter_ch(lambda rows: times_t(rows, down_weight), all_out, core, F32, BF16)

time: 311 us -> 323 us (1.039)
  blocking collectives: 169 us -> 180 us
    all_to_all x0 -> x1, blocking collectives: none -> 29.7 us  [part_skins_by_axis(): lax.all_to_all(jnp.stack([u_in] * lax.axis_size('ch'), 0), 'ch', 0, 0)]
    all_gather x1 -> x0, blocking collectives: 17.1 us -> none  [on_device(): lax.all_gather(hidden_tan, 'ch', axis=0, tiled=True)]
    all_to_all x2, blocking collectives: 54.2 us -> 50.8 us  [scatter_ch(): lax.all_to_all(blocks, 'ch', 0, 0, tiled=True, axis_index_groups=chip_gro...]
where the time goes in v1:
time: 323 us; the launch traced here: 321 us
  blocking collectives  180 us (56%)
  waiting for transfers between devices  54 us (17%)
  matrix products  28.7 us (9%)
  starting transfers between devices  27.8 us (9%)
  between operations  14.6 us (5%)
  other arithmetic  11.1 us (3%)
  local copies, waits for them, and re-layouts  4.92 us (2%)
    all_to_all x2, blocking collectives, scatter_ch(): lax.all_to_all(blocks, 'ch', 0, 0, tiled=True, axis_index_groups=chip_gro...  50.8 us
    all_to_all x2, blocking collectives, scatter_tok(): arrived = lax.all_to_all(blocks, 'tok', 0, 0, tiled=True)  45.9 us
    all_to_all x1, blocking collectives, part_skins_by_axis(): lax.all_to_all(jnp.stack([u_in] * lax.axis_size('ch'), 0), 'ch', 0, 0)  29.7 us
    all_gather x1, blocking collectives, on_device(): lax.all_gather(back, 'ch', axis=0, tiled=True, axis_index_groups=chip_gro...  28.3 us
    all_to_all x2, blocking collectives, gather_tok(): return lax.all_to_all(copies, 'tok', 0, 0, tiled=True)  25.6 us
    ppermute x11, waiting for transfers between devices, swap(): return lax.ppermute(value, 'ch', pairs)  25.3 us
    all_to_all x2, waiting for transfers between devices, gather_tok(): return lax.all_to_all(copies, 'tok', 0, 0, tiled=True)  16.6 us
    ppermute x11, starting transfers between devices, swap(): return lax.ppermute(value, 'ch', pairs)  14.9 us
  transfers between devices with their start and end apart: 14, of which 11 were waited for; matrix products, arithmetic and copies ran while one was open for 5% of the time, Pallas kernels for 0%

profile of v1, /device:TPU:2, one launch (start us, length us, event | category | flops | bytes accessed | tf_op | source)
XLA Modules:
  0.0 321.4 jit_solution(9788505599749150938)
XLA Ops:
  7.2 0.8 add_convert_fusion
  8.0 1.0 multiply_convert_fusion.3
  9.1 0.1 collective-permute-start
  9.2 1.2 collective-permute-done
  10.4 0.9 add_select_fusion.5
  11.2 2.0 collective-permute-start.1
  13.2 2.0 collective-permute-done.1
  15.2 3.4 %collective-permute-start.2 = (bf16[16,1024]{1,0:T(8,128)(2,1)S(1)}, bf16[16,1024]{1,0:T(8,128)(2,1)S(1)}, u32[]{:S(2)}, u32[]{:S(2)}) collective-permute-start(bf16[16,1024]{1,0:T(8,128)(2,1)S(1)} %add_select_fusion.4), channel_id=1, source_target_pairs={{0,4},{1,5},{2,6},{3,7},{4,0},{5,1},{6,2},{7,3},{8,12},{9,13},{10,... | collective-permute-start | bytes 98312 | tf_op jit(solution)/shard_map/ppermute | solution.py:23
  18.6 1.9 collective-permute-done.2
  20.5 6.9 %collective-permute-start.3 = (bf16[16,1024]{1,0:T(8,128)(2,1)S(1)}, bf16[16,1024]{1,0:T(8,128)(2,1)S(1)}, u32[]{:S(2)}, u32[]{:S(2)}) collective-permute-start(bf16[16,1024]{1,0:T(8,128)(2,1)S(1)} %add_select_fusion.3), channel_id=1, source_target_pairs={{0,8},{1,9},{2,10},{3,11},{4,12},{5,13},{6,14},{7,15},{8,0},{9,1},... | collective-permute-start | bytes 98312 | tf_op jit(solution)/shard_map/ppermute | solution.py:23
  27.4 1.6 broadcast_in_dim.10
  29.1 7.5 %all-to-all-start = ((bf16[16,16,1024]{2,1,0:T(8,128)(2,1)}), bf16[16,16,1024]{2,1,0:T(8,128)(2,1)}, u32[]{:S(2)}, u32[]{:S(2)}) async-start(bf16[16,16,1024]{2,1,0:T(8,128)(2,1)} %broadcast_in_dim.10), calls=%async_computation | async-start | bytes 1048576 | tf_op jit(solution)/shard_map/all_to_all | solution.py:54
  36.7 1.0 fusion.14
  37.8 7.6 %all-to-all-done = bf16[16,16,1024]{2,1,0:T(8,128)(2,1)} async-done(((bf16[16,16,1024]{2,1,0:T(8,128)(2,1)}), bf16[16,16,1024]{2,1,0:T(8,128)(2,1)}, u32[]{:S(2)}, u32[]{:S(2)}) %all-to-all-start) | async-done | bytes 524320 | tf_op jit(solution)/shard_map/all_to_all | solution.py:54
  45.4 3.2 %convolution_bitcast_fusion = f32[256,1,1664]{2,0,1:T(8,128)S(1)} fusion(bf16[256,1024]{1,0:T(8,128)(2,1)} %bitcast, bf16[1024,1664]{1,0:T(8,128)(2,1)} %param.11), kind=kOutput, calls=%fused_computation.3 | convolution fusion | flops 872415232 | bytes 5636096 | tf_op jit(solution)/shard_map/dot_general | solution.py:88
  48.7 2.2 convolution_bitcast_fusion.1
  50.8 1.9 pad_maximum_fusion
  52.9 0.8 broadcast_in_dim.11
  53.7 5.4 %all-to-all-start.1 = ((bf16[16,16,1024]{2,1,0:T(8,128)(2,1)}), bf16[16,16,1024]{2,1,0:T(8,128)(2,1)}, u32[]{:S(2)}, u32[]{:S(2)}) async-start(bf16[16,16,1024]{2,1,0:T(8,128)(2,1)} %broadcast_in_dim.11), calls=%async_computation.2 | async-start | bytes 1048576 | tf_op jit(solution)/shard_map/all_to_all | solution.py:54
  59.2 9.0 %all-to-all-done.1 = bf16[16,16,1024]{2,1,0:T(8,128)(2,1)} async-done(((bf16[16,16,1024]{2,1,0:T(8,128)(2,1)}), bf16[16,16,1024]{2,1,0:T(8,128)(2,1)}, u32[]{:S(2)}, u32[]{:S(2)}) %all-to-all-start.1) | async-done | bytes 524320 | tf_op jit(solution)/shard_map/all_to_all | solution.py:54
  68.1 1.1 constant_dynamic-slice_fusion.2
  69.2 2.6 convolution_convert_fusion
  71.9 0.7 convolution_convert_fusion.1
  72.6 0.1 collective-permute-start.4
  72.7 0.7 fusion.15
  73.4 1.2 copy-done.1
  74.5 0.7 fusion.16
  75.2 0.1 fusion.3
  75.3 32.4 %all_to_all.45 = bf16[8,16,3328]{2,1,0:T(8,128)(2,1)S(1)} all-to-all(bf16[8,16,3328]{2,1,0:T(8,128)(2,1)S(1)} %bitcast.72), channel_id=1, replica_groups={{0,2,4,6,8,10,12,14},{1,3,5,7,9,11,13,15},{16,18,20,22,24,26,28,30},{17..., dimensions={0} | all-to-all | bytes 1703936 | tf_op jit(solution)/shard_map/all_to_all | solution.py:83
  107.7 0.8 convert_reduce_fusion
  108.6 12.0 %reduce-scatter.2.cloned.1.call-done = f32[16,2,1664]{2,0,1:T(8,128)} async-done(((f32[256,2,1664]{2,0,1:T(8,128)}), f32[16,2,1664]{2,0,1:T(8,128)}) %reduce-scatter.2.cloned.1.call-update) | async-done | bytes 213008 | tf_op jit(solution)/shard_map/reduce_scatter | solution.py:113
  120.6 1.1 fusion.11
  121.7 0.1 stack.13
  121.8 29.7 %all_to_all.46 = bf16[16,16,1664]{2,1,0:T(8,128)(2,1)S(1)} all-to-all(bf16[16,16,1664]{2,1,0:T(8,128)(2,1)S(1)} %stack.13), channel_id=1, replica_groups=mesh['tok'=16,'ch'=16] {'ch'}, dimensions={0} | all-to-all | bytes 1703936 | tf_op jit(solution)/shard_map/all_to_all | solution.py:99
  151.5 3.1 fusion
  154.7 24.5 %all_to_all.47 = f32[16,16,1024]{2,1,0:T(8,128)} all-to-all(f32[16,16,1024]{2,1,0:T(8,128)S(1)} %fusion), channel_id=1, replica_groups=mesh['tok'=16,'ch'=16] {'tok'}, dimensions={0} | all-to-all | bytes 2097152 | tf_op jit(solution)/shard_map/all_to_all | solution.py:60
  179.1 1.3 reduce_sum.55
  180.5 14.9 %all_to_all.48 = bf16[16,16,1024]{2,1,0:T(8,128)(2,1)S(1)} all-to-all(bf16[16,16,1024]{2,1,0:T(8,128)(2,1)S(1)} %broadcast_in_dim.12), channel_id=1, replica_groups=mesh['tok'=16,'ch'=16] {'tok'}, dimensions={0} | all-to-all | bytes 1048576 | tf_op jit(solution)/shard_map/all_to_all | solution.py:54
  195.4 3.2 fusion.17
  198.6 0.3 collective-permute-start.5
  198.9 2.4 collective-permute-done.5
  201.2 1.2 fusion.2
  202.5 18.4 %all_to_all.49 = bf16[8,16,1664]{2,1,0:T(8,128)(2,1)S(1)} all-to-all(bf16[8,16,1664]{2,1,0:T(8,128)(2,1)S(1)} %bitcast.80), channel_id=1, replica_groups={{0,2,4,6,8,10,12,14},{1,3,5,7,9,11,13,15},{16,18,20,22,24,26,28,30},{17..., dimensions={0} | all-to-all | bytes 851968 | tf_op jit(solution)/shard_map/all_to_all | solution.py:83
  220.9 0.1 multiply_convert_fusion.1
  221.0 28.3 %all_gather.3 = bf16[128,3328]{1,0:T(8,128)(2,1)} all-gather(bf16[16,3328]{1,0:T(8,128)(2,1)S(1)} %pad_maximum_fusion.3), channel_id=1, replica_groups={{0,2,4,6,8,10,12,14},{1,3,5,7,9,11,13,15},{16,18,20,22,24,26,28,30},{17..., dimensions={0}, use_global_device_ids=true | all-gather | bytes 958464 | tf_op jit(solution)/shard_map/all_gather | solution.py:137
  249.3 2.4 fusion.8
  251.7 2.2 convolution_add_fusion.2
  254.0 2.2 fusion.4
  256.2 2.2 broadcast_select_fusion.1
  258.5 0.1 pad_maximum_fusion.1
  258.6 21.4 %all_to_all.50 = f32[16,16,1024]{2,1,0:T(8,128)} all-to-all(f32[16,16,1024]{2,1,0:T(8,128)S(1)} %bitcast.71), channel_id=1, replica_groups=mesh['tok'=16,'ch'=16] {'tok'}, dimensions={0} | all-to-all | bytes 2097152 | tf_op jit(solution)/shard_map/all_to_all | solution.py:60
  280.0 1.3 reduce_sum.57
  281.4 1.0 fusion.18
  282.5 0.1 collective-permute-start.7
  282.6 1.2 collective-permute-done.7
  283.9 0.1 collective-permute-start.8
  284.0 4.3 %collective-permute-done.8 = f32[16,1024]{1,0:T(8,128)S(1)} collective-permute-done((f32[16,1024]{1,0:T(8,128)S(1)}, f32[16,1024]{1,0:T(8,128)S(1)}, u32[]{:S(2)}, u32[]{:S(2)}) %collective-permute-start.8) | collective-permute-done | bytes 65568 | tf_op jit(solution)/shard_map/ppermute | solution.py:23
  288.3 0.3 collective-permute-start.9
  288.6 5.2 %collective-permute-done.9 = f32[16,1024]{1,0:T(8,128)S(1)} collective-permute-done((f32[16,1024]{1,0:T(8,128)S(1)}, f32[16,1024]{1,0:T(8,128)S(1)}, u32[]{:S(2)}, u32[]{:S(2)}) %collective-permute-start.9) | collective-permute-done | bytes 65568 | tf_op jit(solution)/shard_map/ppermute | solution.py:23
  293.8 1.6 collective-permute-start.10
  295.5 7.1 %collective-permute-done.10 = f32[16,1024]{1,0:T(8,128)S(1)} collective-permute-done((f32[16,1024]{1,0:T(8,128)S(1)}, f32[16,1024]{1,0:T(8,128)S(1)}, u32[]{:S(2)}, u32[]{:S(2)}) %collective-permute-start.10) | collective-permute-done | bytes 65568 | tf_op jit(solution)/shard_map/ppermute | solution.py:23
  302.6 0.7 multiply_reduce_fusion
  303.3 10.7 %all_to_all.51 = f32[16,8,128]{2,1,0:T(8,128)S(1)} all-to-all(f32[16,8,128]{2,1,0:T(8,128)S(1)} %broadcast_in_dim.14), channel_id=1, replica_groups=mesh['tok'=16,'ch'=16] {'tok'}, dimensions={0} | all-to-all | bytes 131072 | tf_op jit(solution)/shard_map/all_to_all | solution.py:54
  314.0 0.6 multiply_bitcast_fusion
  (66 shorter events, 0.6 us)
Async XLA Ops:
  7.2 41.5 %copy-start = (bf16[1024,1664]{1,0:T(8,128)(2,1)S(1)}, bf16[1024,1664]{1,0:T(8,128)(2,1)}, u32[]{:S(2)}) copy-start(bf16[1024,1664]{1,0:T(8,128)(2,1)} %param.10) | copy-start | bytes 10223620
  9.1 1.3 collective-permute-start
  11.2 4.0 %collective-permute-start.1 = (bf16[16,1024]{1,0:T(8,128)(2,1)S(1)}, bf16[16,1024]{1,0:T(8,128)(2,1)S(1)}, u32[]{:S(2)}, u32[]{:S(2)}) collective-permute-start(bf16[16,1024]{1,0:T(8,128)(2,1)S(1)} %add_select_fusion.5), channel_id=1, source_target_pairs={{0,2},{1,3},{2,0},{3,1},{4,6},{5,7},{6,4},{7,5},{8,10},{9,11},{10,... | collective-permute-start | bytes 98312 | tf_op jit(solution)/shard_map/ppermute | solution.py:23
  15.2 5.3 %collective-permute-start.2 = (bf16[16,1024]{1,0:T(8,128)(2,1)S(1)}, bf16[16,1024]{1,0:T(8,128)(2,1)S(1)}, u32[]{:S(2)}, u32[]{:S(2)}) collective-permute-start(bf16[16,1024]{1,0:T(8,128)(2,1)S(1)} %add_select_fusion.4), channel_id=1, source_target_pairs={{0,4},{1,5},{2,6},{3,7},{4,0},{5,1},{6,2},{7,3},{8,12},{9,13},{10,... | collective-permute-start | bytes 98312 | tf_op jit(solution)/shard_map/ppermute | solution.py:23
  20.5 16.1 %collective-permute-start.3 = (bf16[16,1024]{1,0:T(8,128)(2,1)S(1)}, bf16[16,1024]{1,0:T(8,128)(2,1)S(1)}, u32[]{:S(2)}, u32[]{:S(2)}) collective-permute-start(bf16[16,1024]{1,0:T(8,128)(2,1)S(1)} %add_select_fusion.3), channel_id=1, source_target_pairs={{0,8},{1,9},{2,10},{3,11},{4,12},{5,13},{6,14},{7,15},{8,0},{9,1},... | collective-permute-start | bytes 98312 | tf_op jit(solution)/shard_map/ppermute | solution.py:23
  29.1 16.4 %all-to-all-start = ((bf16[16,16,1024]{2,1,0:T(8,128)(2,1)}), bf16[16,16,1024]{2,1,0:T(8,128)(2,1)}, u32[]{:S(2)}, u32[]{:S(2)}) async-start(bf16[16,16,1024]{2,1,0:T(8,128)(2,1)} %broadcast_in_dim.10), calls=%async_computation | async-start | bytes 1048576 | tf_op jit(solution)/shard_map/all_to_all | solution.py:54
  36.5 84.1 %reduce-scatter.2.cloned.1.call-start = ((), (), s32[]{:S(2)}) async-start(), calls=%async_computation.10 | async-start | bytes 3620864 | tf_op jit(solution)/shard_map/reduce_scatter | solution.py:113
  53.7 14.4 %all-to-all-start.1 = ((bf16[16,16,1024]{2,1,0:T(8,128)(2,1)}), bf16[16,16,1024]{2,1,0:T(8,128)(2,1)}, u32[]{:S(2)}, u32[]{:S(2)}) async-start(bf16[16,16,1024]{2,1,0:T(8,128)(2,1)} %broadcast_in_dim.11), calls=%async_computation.2 | async-start | bytes 1048576 | tf_op jit(solution)/shard_map/all_to_all | solution.py:54
  72.5 2.0 copy-start.1
  72.6 2.6 collective-permute-start.4
  180.5 20.8 %copy-start.3 = (bf16[1664,1024]{1,0:T(8,128)(2,1)S(1)}, bf16[1664,1024]{1,0:T(8,128)(2,1)}, u32[]{:S(2)}) copy-start(bf16[1664,1024]{1,0:T(8,128)(2,1)} %param.12) | copy-start | bytes 10223620
  198.6 22.3 %copy-start.4 = (f32[16,2,1664]{2,0,1:T(8,128)S(1)}, f32[16,2,1664]{2,0,1:T(8,128)}, u32[]{:S(2)}) copy-start(f32[16,2,1664]{2,0,1:T(8,128)} %reduce-scatter.2.cloned.1.call-done) | copy-start | bytes 638980
  198.6 2.6 collective-permute-start.5
  249.3 4.6 %collective-permute-start.6 = (bf16[128,3328]{1,0:T(8,128)(2,1)}, bf16[128,3328]{1,0:T(8,128)(2,1)}, u32[]{:S(2)}, u32[]{:S(2)}) collective-permute-start(bf16[128,3328]{1,0:T(8,128)(2,1)} %all_gather.3), channel_id=1, source_target_pairs={{0,1},{1,0},{2,3},{3,2},{4,5},{5,4},{6,7},{7,6},{8,9},{9,8},{10,11... | collective-permute-start | bytes 2555912 | tf_op jit(solution)/shard_map/ppermute | solution.py:23
  249.3 2.4 copy-start.2
  258.5 37.0 %copy-start.6 = (s32[1024]{0:T(1024)S(1)}, s32[1024]{0:T(1024)}, u32[]{:S(2)}) copy-start(s32[1024]{0:T(1024)} %param.9) | copy-start | bytes 12292
  258.5 44.1 %copy-start.5 = (s32[16,1024]{1,0:T(8,128)S(1)}, s32[16,1024]{1,0:T(8,128)}, u32[]{:S(2)}) copy-start(s32[16,1024]{1,0:T(8,128)} %param.8) | copy-start | bytes 196612
  282.5 1.3 collective-permute-start.7
  283.9 4.4 %collective-permute-start.8 = (f32[16,1024]{1,0:T(8,128)S(1)}, f32[16,1024]{1,0:T(8,128)S(1)}, u32[]{:S(2)}, u32[]{:S(2)}) collective-permute-start(f32[16,1024]{1,0:T(8,128)S(1)} %add_select_fusion.2), channel_id=1, source_target_pairs={{0,2},{1,3},{2,0},{3,1},{4,6},{5,7},{6,4},{7,5},{8,10},{9,11},{10,... | collective-permute-start | bytes 196616 | tf_op jit(solution)/shard_map/ppermute | solution.py:23
  288.3 5.6 %collective-permute-start.9 = (f32[16,1024]{1,0:T(8,128)S(1)}, f32[16,1024]{1,0:T(8,128)S(1)}, u32[]{:S(2)}, u32[]{:S(2)}) collective-permute-start(f32[16,1024]{1,0:T(8,128)S(1)} %add_select_fusion.1), channel_id=1, source_target_pairs={{0,4},{1,5},{2,6},{3,7},{4,0},{5,1},{6,2},{7,3},{8,12},{9,13},{10,... | collective-permute-start | bytes 196616 | tf_op jit(solution)/shard_map/ppermute | solution.py:23
  293.8 8.8 %collective-permute-start.10 = (f32[16,1024]{1,0:T(8,128)S(1)}, f32[16,1024]{1,0:T(8,128)S(1)}, u32[]{:S(2)}, u32[]{:S(2)}) collective-permute-start(f32[16,1024]{1,0:T(8,128)S(1)} %add_select_fusion), channel_id=1, source_target_pairs={{0,8},{1,9},{2,10},{3,11},{4,12},{5,13},{6,14},{7,15},{8,0},{9,1},... | collective-permute-start | bytes 196616 | tf_op jit(solution)/shard_map/ppermute | solution.py:23
Sparse Core Ops, SparseCore 0:
  52.9 67.6 reduce-scatter.1
